TPU v7x, 32 devices: a whole 2x2x4 slice. The times are simulated.
32 devices in a mesh: dp: 8 (over y, x, core), tensor: 4 (over z).
Axes of the slice: x: 2, y: 2, z: 4, core: 2. Of those that a mesh axis runs over, the one named last changes fastest.
Arguments:
- inputs: bfloat16 [16384, 768], P('dp'), may hold values from -6 to 6
- w_query: bfloat16 [768, 768], P(None, 'tensor'), may hold values from -0.21875 to 0.21875
- b_query: bfloat16 [768], P('tensor'), may hold values from -3 to 3
- w_key: bfloat16 [768, 768], P(None, 'tensor'), may hold values from -0.21875 to 0.21875
- w_value: bfloat16 [768, 768], P(None, 'tensor'), may hold values from -0.21875 to 0.21875
- b_value: bfloat16 [768], P('tensor'), may hold values from -3 to 3
- w_output: bfloat16 [768, 768], P('tensor'), may hold values from -6 to 6
- b_output: bfloat16 [768], replicated, may hold values from -3 to 3
- gain_attn: bfloat16 [768], replicated, may hold values from 0.5 to 1.5
- shift_attn: bfloat16 [768], replicated, may hold values from -3 to 3
- w_inner: bfloat16 [768, 3072], P(None, 'tensor'), may hold values from -0.21875 to 0.21875
- b_inner: bfloat16 [3072], P('tensor'), may hold values from -3 to 3
- w_outer: bfloat16 [3072, 768], P('tensor'), may hold values from -0.109375 to 0.109375
- b_outer: bfloat16 [768], replicated, may hold values from -3 to 3
- gain_ffn: bfloat16 [768], replicated, may hold values from 0.5 to 1.5
- shift_ffn: bfloat16 [768], replicated, may hold values from -3 to 3
- cotangent: bfloat16 [16384, 768], P('dp'), may hold values from -6 to 6
Outputs:
- layer_out: bfloat16 [16384, 768], P('dp')
- grad_inputs: float32 [16384, 768], P('dp')
- grad_w_query: float32 [768, 768], P('dp', 'tensor')
- grad_b_query: float32 [768], P('tensor')
- grad_w_key: float32 [768, 768], P('dp', 'tensor')
- grad_w_value: float32 [768, 768], P('dp', 'tensor')
- grad_b_value: float32 [768], P('tensor')
- grad_w_output: float32 [768, 768], P('tensor', 'dp')
- grad_b_output: float32 [768], replicated
- grad_gain_attn: float32 [768], replicated
- grad_shift_attn: float32 [768], replicated
- grad_w_inner: float32 [768, 3072], P('dp', 'tensor')
- grad_b_inner: float32 [3072], P('tensor')
- grad_w_outer: float32 [3072, 768], P('tensor', 'dp')
- grad_b_outer: float32 [768], replicated
- grad_gain_ffn: float32 [768], replicated
- grad_shift_ffn: float32 [768], replicated
All inputs are finite; a program needn't handle non-finite values.
Results may differ from a plain program's by a relative error of at most 0.014.
Values sent between devices are 32-bit elements; how exact they have to be, the bound alone decides.
No kernel may reach another device: no remote copies, remote signals or barrier semaphores. Data moves between devices by JAX's collectives and lax.ppermute only.
A program may use at most 128 MiB of HBM per device.

v0:
```python
from functools import partial
import jax
import jax.numpy as jnp
from jax import lax
from jax.sharding import PartitionSpec as P

HEAD_DIM = 64
LENGTH = 512
EPSILON = 1e-12


def norm_forward(values, gain, shift):
    center = values - jnp.mean(values, axis=-1, keepdims=True)
    inverse = lax.rsqrt(jnp.mean(center * center, axis=-1, keepdims=True) + EPSILON)
    normed = center * inverse
    return (normed * gain + shift, normed, inverse)


def norm_backward(upstream, gain, normed, inverse):
    scaled = upstream * gain
    first_mean = jnp.mean(scaled, axis=-1, keepdims=True)
    cross_mean = jnp.mean(scaled * normed, axis=-1, keepdims=True)
    grad_values = inverse * (scaled - first_mean - normed * cross_mean)
    return (grad_values, jnp.sum(upstream * normed, axis=0), jnp.sum(upstream, axis=0))


def contract_rows(left, right):
    return lax.dot_general(
        left, right, (((0,), (0,)), ((), ())), preferred_element_type=jnp.float32
    )


def times_transpose(left, right):
    return lax.dot_general(
        left, right, (((1,), (1,)), ((), ())), preferred_element_type=jnp.float32
    )


def column_sums(values):
    return jnp.sum(values.astype(jnp.float32), axis=0)


def attend_forward(query_seq, key_seq, value_seq, block_rows, scale):
    length, heads_here, head_size = query_seq.shape

    def one_block(query_block):
        scores = (
            jnp.einsum("qhd,khd->hqk", query_block, key_seq, preferred_element_type=jnp.float32)
            * scale
        )
        largest = jnp.max(scores, axis=-1, keepdims=True)
        expon = jnp.exp(scores - largest)
        totals = jnp.sum(expon, axis=-1, keepdims=True)
        probs = (expon / totals).astype(jnp.bfloat16)
        context = jnp.einsum("hqk,khd->qhd", probs, value_seq, preferred_element_type=jnp.float32)
        return (context.astype(jnp.bfloat16), largest[..., 0] + jnp.log(totals[..., 0]))

    blocks = query_seq.reshape(length // block_rows, block_rows, heads_here, head_size)
    context, log_totals = lax.map(one_block, blocks)
    return (context.reshape(length, heads_here * head_size), log_totals)


def attend_backward(query_seq, key_seq, value_seq, grad_context, log_totals, block_rows, scale):
    length, heads_here, head_size = query_seq.shape
    block_shape = (length // block_rows, block_rows, heads_here, head_size)

    def step(carry, pieces):
        grad_keys, grad_values = carry
        query_block, grad_block, lse_block = pieces
        scores = (
            jnp.einsum("qhd,khd->hqk", query_block, key_seq, preferred_element_type=jnp.float32)
            * scale
        )
        probs = jnp.exp(scores - lse_block[..., None])
        grad_values = grad_values + jnp.einsum(
            "hqk,qhd->khd",
            probs.astype(jnp.bfloat16),
            grad_block,
            preferred_element_type=jnp.float32,
        )
        grad_probs = jnp.einsum(
            "qhd,khd->hqk", grad_block, value_seq, preferred_element_type=jnp.float32
        )
        row_terms = jnp.sum(probs * grad_probs, axis=-1, keepdims=True)
        grad_scores = (probs * (grad_probs - row_terms)).astype(jnp.bfloat16)
        grad_query = (
            jnp.einsum("hqk,khd->qhd", grad_scores, key_seq, preferred_element_type=jnp.float32)
            * scale
        )
        grad_keys = (
            grad_keys
            + jnp.einsum(
                "hqk,qhd->khd", grad_scores, query_block, preferred_element_type=jnp.float32
            )
            * scale
        )
        return ((grad_keys, grad_values), grad_query.astype(jnp.bfloat16))

    zeros_init = jnp.zeros(key_seq.shape, jnp.float32)
    (grad_keys, grad_values), grad_query = lax.scan(
        step,
        (zeros_init, zeros_init),
        (query_seq.reshape(block_shape), grad_context.reshape(block_shape), log_totals),
    )
    flat = (length, heads_here * head_size)
    return (
        grad_query.reshape(flat),
        grad_keys.astype(jnp.bfloat16).reshape(flat),
        grad_values.astype(jnp.bfloat16).reshape(flat),
    )


def shards(
    inputs,
    w_query,
    b_query,
    w_key,
    w_value,
    b_value,
    w_output,
    b_output,
    gain_attn,
    shift_attn,
    w_inner,
    b_inner,
    w_outer,
    b_outer,
    gain_ffn,
    shift_ffn,
    cotangent,
):
    tok_rows = inputs.shape[0]
    heads_here = w_query.shape[1] // HEAD_DIM
    block_rows = min(512, LENGTH)
    scale = HEAD_DIM ** (-0.5)
    split_shape = (tok_rows // LENGTH, LENGTH, heads_here, HEAD_DIM)
    queries = (
        jnp.dot(inputs, w_query, preferred_element_type=jnp.float32) + b_query.astype(jnp.float32)
    ).astype(jnp.bfloat16)
    key_rows = jnp.dot(inputs, w_key, preferred_element_type=jnp.float32).astype(jnp.bfloat16)
    value_rows = (
        jnp.dot(inputs, w_value, preferred_element_type=jnp.float32) + b_value.astype(jnp.float32)
    ).astype(jnp.bfloat16)
    query_split = queries.reshape(split_shape)
    key_split = key_rows.reshape(split_shape)
    value_split = value_rows.reshape(split_shape)

    def forward_seq(triple):
        return attend_forward(triple[0], triple[1], triple[2], block_rows, scale)

    context, log_totals = lax.map(forward_seq, (query_split, key_split, value_split))
    context = context.reshape(tok_rows, heads_here * HEAD_DIM)
    attn_part = jnp.dot(context, w_output, preferred_element_type=jnp.float32)
    attn_total = lax.psum(attn_part, "tensor") + b_output.astype(jnp.float32)
    gain_one = gain_attn.astype(jnp.float32)
    gain_two = gain_ffn.astype(jnp.float32)
    hidden, normed_attn, inverse_attn = norm_forward(
        inputs.astype(jnp.float32) + attn_total, gain_one, shift_attn.astype(jnp.float32)
    )
    hidden_bf = hidden.astype(jnp.bfloat16)
    inner = jnp.dot(hidden_bf, w_inner, preferred_element_type=jnp.float32) + b_inner.astype(
        jnp.float32
    )
    active, gelu_pull = jax.vjp(partial(jax.nn.gelu, approximate=False), inner)
    active_bf = active.astype(jnp.bfloat16)
    outer_part = jnp.dot(active_bf, w_outer, preferred_element_type=jnp.float32)
    outer_total = lax.psum(outer_part, "tensor") + b_outer.astype(jnp.float32)
    layer_out, normed_ffn, inverse_ffn = norm_forward(
        hidden + outer_total, gain_two, shift_ffn.astype(jnp.float32)
    )
    grad_resid2, grad_gain_ffn, grad_shift_ffn = norm_backward(
        cotangent.astype(jnp.float32), gain_two, normed_ffn, inverse_ffn
    )
    grad_outer = grad_resid2.astype(jnp.bfloat16)
    grad_b_outer = column_sums(grad_outer)
    grad_w_outer = contract_rows(active_bf, grad_outer)
    grad_active = times_transpose(grad_outer, w_outer)
    grad_inner = gelu_pull(grad_active)[0].astype(jnp.bfloat16)
    grad_b_inner = column_sums(grad_inner)
    grad_w_inner = contract_rows(hidden_bf, grad_inner)
    grad_hidden = grad_resid2 + lax.psum(times_transpose(grad_inner, w_inner), "tensor")
    grad_resid1, grad_gain_attn, grad_shift_attn = norm_backward(
        grad_hidden, gain_one, normed_attn, inverse_attn
    )
    grad_attn = grad_resid1.astype(jnp.bfloat16)
    grad_b_output = column_sums(grad_attn)
    grad_w_output = contract_rows(context, grad_attn)
    grad_context = times_transpose(grad_attn, w_output).astype(jnp.bfloat16)

    def backward_seq(pieces):
        return attend_backward(
            pieces[0], pieces[1], pieces[2], pieces[3], pieces[4], block_rows, scale
        )

    grad_query, grad_key, grad_value = lax.map(
        backward_seq,
        (query_split, key_split, value_split, grad_context.reshape(split_shape), log_totals),
    )
    flat_shape = (tok_rows, heads_here * HEAD_DIM)
    grad_query = grad_query.reshape(flat_shape)
    grad_key = grad_key.reshape(flat_shape)
    grad_value = grad_value.reshape(flat_shape)
    grad_b_query = column_sums(grad_query)
    grad_b_value = column_sums(grad_value)
    grad_w_query = contract_rows(inputs, grad_query)
    grad_w_key = contract_rows(inputs, grad_key)
    grad_w_value = contract_rows(inputs, grad_value)
    input_part = (
        times_transpose(grad_query, w_query)
        + times_transpose(grad_key, w_key)
        + times_transpose(grad_value, w_value)
    )
    grad_inputs = grad_resid1 + lax.psum(input_part, "tensor")
    small_sums = lax.psum(
        (
            grad_b_query,
            grad_b_value,
            grad_b_output,
            grad_gain_attn,
            grad_shift_attn,
            grad_b_inner,
            grad_b_outer,
            grad_gain_ffn,
            grad_shift_ffn,
        ),
        "dp",
    )
    weight_shards = (
        lax.psum_scatter(grad_w_query, "dp", scatter_dimension=0, tiled=True),
        lax.psum_scatter(grad_w_key, "dp", scatter_dimension=0, tiled=True),
        lax.psum_scatter(grad_w_value, "dp", scatter_dimension=0, tiled=True),
        lax.psum_scatter(grad_w_output, "dp", scatter_dimension=1, tiled=True),
        lax.psum_scatter(grad_w_inner, "dp", scatter_dimension=0, tiled=True),
        lax.psum_scatter(grad_w_outer, "dp", scatter_dimension=1, tiled=True),
    )
    return (
        layer_out.astype(jnp.bfloat16),
        grad_inputs,
        weight_shards[0],
        small_sums[0],
        weight_shards[1],
        weight_shards[2],
        small_sums[1],
        weight_shards[3],
        small_sums[2],
        small_sums[3],
        small_sums[4],
        weight_shards[4],
        small_sums[5],
        weight_shards[5],
        small_sums[6],
        small_sums[7],
        small_sums[8],
    )


def solution(mesh):
    in_specs = (
        P("dp", None),
        P(None, "tensor"),
        P("tensor"),
        P(None, "tensor"),
        P(None, "tensor"),
        P("tensor"),
        P("tensor", None),
        P(),
        P(),
        P(),
        P(None, "tensor"),
        P("tensor"),
        P("tensor", None),
        P(),
        P(),
        P(),
        P("dp", None),
    )
    out_specs = (
        P("dp", None),
        P("dp", None),
        P("dp", "tensor"),
        P("tensor"),
        P("dp", "tensor"),
        P("dp", "tensor"),
        P("tensor"),
        P("tensor", "dp"),
        P(),
        P(),
        P(),
        P("dp", "tensor"),
        P("tensor"),
        P("tensor", "dp"),
        P(),
        P(),
        P(),
    )
    return jax.shard_map(shards, mesh=mesh, in_specs=in_specs, out_specs=out_specs, check_vma=False)
```

profile of v0, /device:TPU:0, one launch (start us, length us, event | category | flops | bytes accessed | tf_op | source)
XLA Modules:
  0.0 1302.5 jit_solution(1890085184275890445)
XLA Ops:
  22.4 13.0 while.10
  37.6 4.7 fusion.73
  45.1 222.9 %all-reduce.6.cloned.1.call-done = f32[2048,768]{1,0:T(8,128)} async-done(((f32[2048,768]{1,0:T(8,128)}), f32[2048,768]{1,0:T(8,128)}) %all-reduce.6.cloned.1.call-update) | async-done | bytes 6291472 | tf_op jit(solution)/shard_map/psum | solution.py:154
  268.0 4.6 fusion.72
  275.3 18.3 %multiply_convert_fusion.1 = (bf16[2048,768]{1,0:T(8,128)(2,1)S(1)}, f32[2048,768]{1,0:T(8,128)}, f32[2048,768]{1,0:T(8,128)}) fusion(f32[768]{0:T(1024)S(1)} %copy-done.32, bf16[2048,768]{1,0:T(8,128)(2,1)S(1)} %fusion.58, bf16[768,768]{1,0:T(8,128)(2,1)S(1)} %copy-done), kind=kOutput, calls=%fused_computation.79 | convolution fusion | flops 2519728128 | bytes 20057088 | tf_op jit(solution)/shard_map/dot_general | solution.py:161
  304.2 217.6 %all-reduce.8.cloned.1.call-done = f32[2048,768]{1,0:T(8,128)} async-done(((f32[2048,768]{1,0:T(8,128)}), f32[2048,768]{1,0:T(8,128)}) %all-reduce.8.cloned.1.call-update) | async-done | bytes 6291472 | tf_op jit(solution)/shard_map/psum | solution.py:167
  521.8 5.7 fusion.70
  537.5 9.5 convert_reduce_fusion.2
  548.7 4.5 fusion.75
  553.5 221.7 %all-reduce.10.cloned.1.call-done = f32[2048,768]{1,0:T(8,128)} async-done(((f32[2048,768]{1,0:T(8,128)}), f32[2048,768]{1,0:T(8,128)}) %all-reduce.10.cloned.1.call-update) | async-done | bytes 6291472 | tf_op jit(solution)/shard_map/psum | solution.py:181
  775.2 8.7 multiply_reduce_fusion.2
  784.0 5.2 convert_reduce_fusion.3
  796.9 25.6 %while.27 = (s32[]{:T(128)}, bf16[4,512,192]{1,2,0:T(8,128)(2,1)S(1)}, bf16[4,512,192]{1,2,0:T(8,128)(2,1)}, bf16[4,512,192]{1,2,0:T(8,128)(2,1)}, bf16[4,512,3,...) while((s32[]{:T(128)}, ...), condition=%wide.region_17.18_spmd, body=%wide.region_15.17_spmd.sunk | while | flops 513243648 | bytes 26788472 | solution.py:195
  822.7 5.3 fusion.76
  835.7 8.0 fusion.63
  843.8 7.0 fusion.78
  865.2 25.8 %all-reduce = (f32[192]{0:T(256)}, f32[192]{0:T(256)}, f32[768]{0:T(1024)}, f32[768]{0:T(1024)}, f32[768]{0:T(1024)}, /*index=5*/f32[768]{0:T(1024)}, f32[768]{0:T(1024)}, f32[768]{0:T(1024)}, f32[768]{0:T(1024)}) all-reduce(f32[192]{0:T(256)S(1)} %convert_reduce_fusion.5, ...), channel_id=1, replica_groups=mesh['dp'=8,'tensor'=4] {'dp'}, use_global_device_ids=true, to_apply=%region_21.22 | all-reduce | flops 5760 | bytes 46080 | tf_op jit(solution)/shard_map/psum | solution.py:214
  892.8 194.5 %all-reduce.12.cloned.1.call-done = f32[2048,768]{1,0:T(8,128)} async-done(((f32[2048,768]{1,0:T(8,128)}), f32[2048,768]{1,0:T(8,128)}) %all-reduce.12.cloned.1.call-update) | async-done | bytes 6291472 | tf_op jit(solution)/shard_map/psum | solution.py:213
  1087.3 8.1 add.177
  1095.4 37.2 %reduce-scatter.17.cloned.1.call-done = f32[768,96]{0,1:T(8,128)} async-done(((f32[768,768]{0,1:T(8,128)}), f32[768,96]{0,1:T(8,128)}) %reduce-scatter.17.cloned.1.call-update) | async-done | bytes 294928 | tf_op jit(solution)/shard_map/reduce_scatter | solution.py:234
  1132.5 46.8 %reduce-scatter.15.cloned.1.call-done = f32[96,768]{1,0:T(8,128)} async-done(((f32[768,768]{1,0:T(8,128)}), f32[96,768]{1,0:T(8,128)}) %reduce-scatter.15.cloned.1.call-update) | async-done | bytes 294928 | tf_op jit(solution)/shard_map/reduce_scatter | solution.py:233
  1179.3 38.7 %reduce-scatter.19.cloned.1.call-done = f32[96,192]{1,0:T(8,128)} async-done(((f32[768,192]{1,0:T(8,128)}), f32[96,192]{1,0:T(8,128)}) %reduce-scatter.19.cloned.1.call-update) | async-done | bytes 73744
  1218.1 38.8 %reduce-scatter.21.cloned.1.call-done = f32[96,192]{1,0:T(8,128)} async-done(((f32[768,192]{1,0:T(8,128)}), f32[96,192]{1,0:T(8,128)}) %reduce-scatter.21.cloned.1.call-update) | async-done | bytes 73744
  1256.8 38.6 %reduce-scatter.23.cloned.1.call-done = f32[96,192]{1,0:T(8,128)} async-done(((f32[768,192]{1,0:T(8,128)}), f32[96,192]{1,0:T(8,128)}) %reduce-scatter.23.cloned.1.call-update) | async-done | bytes 73744
  (226 shorter events, 115.0 us)
Async XLA Ops:
  7.2 268.1 %copy-start = (bf16[768,768]{1,0:T(8,128)(2,1)S(1)}, bf16[768,768]{1,0:T(8,128)(2,1)}, u32[]{:S(2)}) copy-start(bf16[768,768]{1,0:T(8,128)(2,1)} %param.31) | copy-start | bytes 3538948
  7.2 260.8 %all-reduce.6.cloned.1.call-start = ((), (), s32[]{:S(2)}) async-start(), calls=%async_computation.6 | async-start | bytes 12582912 | tf_op jit(solution)/shard_map/psum | solution.py:154
  42.3 479.5 %all-reduce.8.cloned.1.call-start = ((), (), s32[]{:S(2)}) async-start(), calls=%async_computation.7 | async-start | bytes 12582912 | tf_op jit(solution)/shard_map/psum | solution.py:167
  275.3 18.3 %copy-start.16 = (bf16[2048,768]{1,0:T(8,128)(2,1)}, bf16[2048,768]{1,0:T(8,128)(2,1)S(1)}, u32[]{:S(2)}) copy-start(bf16[2048,768]{1,0:T(8,128)(2,1)S(1)} %fusion.58) | copy-start | bytes 9437188
  275.3 20.1 %copy-start.37 = (bf16[768,768]{1,0:T(8,128)(2,1)S(1)}, bf16[768,768]{1,0:T(8,128)(2,1)}, u32[]{:S(2)}) copy-start(bf16[768,768]{1,0:T(8,128)(2,1)} %param.33) | copy-start | bytes 3538948
  299.8 475.4 %all-reduce.10.cloned.1.call-start = ((), (), s32[]{:S(2)}) async-start(), calls=%async_computation.8 | async-start | bytes 12582912 | tf_op jit(solution)/shard_map/psum | solution.py:181
  529.4 8.1 slice-start.2
  537.5 9.5 copy-start.4
  553.3 222.0 %copy-start.21 = (f32[768]{0:T(1024)S(1)}, f32[768]{0:T(1024)}, u32[]{:S(2)}) copy-start(f32[768]{0:T(1024)} %convert_element_type.125) | copy-start | bytes 9220
  553.3 337.7 %reduce-scatter.25.cloned.1.call-start = ((), (), s32[]{:S(2)}) async-start(), calls=%async_computation.15 | async-start | bytes 884736
  828.1 259.2 %all-reduce.12.cloned.1.call-start = ((), (), s32[]{:S(2)}) async-start(), calls=%async_computation.9 | async-start | bytes 12582912 | tf_op jit(solution)/shard_map/psum | solution.py:213
  835.4 297.1 %reduce-scatter.17.cloned.1.call-start = ((), (), s32[]{:S(2)}) async-start(), calls=%async_computation.11 | async-start | bytes 2654208 | tf_op jit(solution)/shard_map/reduce_scatter | solution.py:234
  843.7 7.1 copy-start.7
  843.7 335.6 %reduce-scatter.15.cloned.1.call-start = ((), (), s32[]{:S(2)}) async-start(), calls=%async_computation.10 | async-start | bytes 2654208 | tf_op jit(solution)/shard_map/reduce_scatter | solution.py:233
  850.8 10.1 copy-start.9
  850.8 367.3 %reduce-scatter.19.cloned.1.call-start = ((), (), s32[]{:S(2)}) async-start(), calls=%async_computation.12 | async-start | bytes 884736
  854.8 10.0 copy-start.13
  854.8 10.2 copy-start.11
  854.8 402.0 %reduce-scatter.21.cloned.1.call-start = ((), (), s32[]{:S(2)}) async-start(), calls=%async_computation.13 | async-start | bytes 884736
  858.5 6.7 copy-start.28
  858.5 6.7 copy-start.29
  858.5 6.7 copy-start.31
  860.8 434.6 %reduce-scatter.23.cloned.1.call-start = ((), (), s32[]{:S(2)}) async-start(), calls=%async_computation.14 | async-start | bytes 884736
  891.0 404.4 %copy-start.1 = (bf16[768,768]{1,0:T(8,128)(2,1)S(1)}, bf16[768,768]{1,0:T(8,128)(2,1)}, u32[]{:S(2)}) copy-start(bf16[768,768]{1,0:T(8,128)(2,1)} %param.31) | copy-start | bytes 3538948
  (32 other events, 119.6 us)
Sparse Core Ops, SparseCore 0:
  42.4 225.5 all-reduce.5
  300.0 221.7 all-reduce.7
  553.4 221.7 all-reduce.9
  828.2 33.9 reduce-scatter.24
  864.4 222.8 all-reduce.11
  1091.0 41.4 reduce-scatter.16
  1136.8 42.4 reduce-scatter.14
  1183.1 34.9 reduce-scatter.18
  1221.8 34.9 reduce-scatter.20
  1260.4 34.9 reduce-scatter.22
where the time goes:
time: 1310 us; the launch traced here: 1300 us
  waiting for transfers between devices  1060 us (81%)
  matrix products  110 us (8%)
  other arithmetic  58.7 us (4%)
  local copies, waits for them, and re-layouts  34.2 us (3%)
  blocking collectives  25.8 us (2%)
  between operations  15.1 us (1%)
    psum x1, waiting for transfers between devices, shards(): attn_total = lax.psum(attn_part, 'tensor') + b_output.astype(jnp.float32)  223 us
    psum x1, waiting for transfers between devices, shards(): lax.psum(times_transpose(grad_inner, w_inner), 'tensor')  222 us
    psum x1, waiting for transfers between devices, shards(): outer_total = lax.psum(outer_part, 'tensor') + b_outer.astype(jnp.float32)  218 us
    psum x1, waiting for transfers between devices, shards(): grad_inputs = grad_resid1 + lax.psum(input_part, 'tensor')  194 us
    unnamed x14, waiting for transfers between devices  116 us
    reduce_scatter x1, waiting for transfers between devices, shards(): lax.psum_scatter(grad_w_inner, 'dp', scatter_dimension=0, tiled=True)  46.8 us
    reduce_scatter x1, waiting for transfers between devices, shards(): lax.psum_scatter(grad_w_outer, 'dp', scatter_dimension=1, tiled=True)  37.2 us
  transfers between devices with their start and end apart: 10, of which 9 were waited for; matrix products, arithmetic and copies ran while one was open for 4% of the time, Pallas kernels for 0%

commit v1 on v0

--- a/solution.py
+++ b/solution.py
@@ -7,6 +7,11 @@
 HEAD_DIM = 64
 LENGTH = 512
 EPSILON = 1e-12
+
+
+def add_all(value, name):
+    pieces = lax.all_gather(value, name)
+    return jnp.sum(pieces, axis=0)
 
 
 def norm_forward(values, gain, shift):
@@ -178,7 +183,7 @@
     grad_inner = gelu_pull(grad_active)[0].astype(jnp.bfloat16)
     grad_b_inner = column_sums(grad_inner)
     grad_w_inner = contract_rows(hidden_bf, grad_inner)
-    grad_hidden = grad_resid2 + lax.psum(times_transpose(grad_inner, w_inner), "tensor")
+    grad_hidden = grad_resid2 + add_all(times_transpose(grad_inner, w_inner), "tensor")
     grad_resid1, grad_gain_attn, grad_shift_attn = norm_backward(
         grad_hidden, gain_one, normed_attn, inverse_attn
     )

time: 1310 us -> 1500 us (1.15)
  waiting for transfers between devices: 1060 us -> 1230 us
    all_gather x0 -> x1, waiting for transfers between devices: none -> 424 us  [add_all(): pieces = lax.all_gather(value, name)]
    psum x1 -> x0, waiting for transfers between devices: 222 us -> none  [shards(): lax.psum(times_transpose(grad_inner, w_inner), 'tensor')]
    psum x1, waiting for transfers between devices: 194 us -> 162 us  [shards(): grad_inputs = grad_resid1 + lax.psum(input_part, 'tensor')]
  transfers between devices with their start and end apart: 10 -> 10, of which waited for: 9 -> 9; matrix products, arithmetic and copies ran while one was open for 4% -> 6% of each run, Pallas kernels for 0% -> 0%
where the time goes in v1:
time: 1500 us; the launch traced here: 1490 us
  waiting for transfers between devices  1230 us (82%)
  matrix products  109 us (7%)
  other arithmetic  70.2 us (5%)
  local copies, waits for them, and re-layouts  42.3 us (3%)
  blocking collectives  26.5 us (2%)
    all_gather x1, waiting for transfers between devices, add_all(): pieces = lax.all_gather(value, name)  424 us
    psum x1, waiting for transfers between devices, shards(): attn_total = lax.psum(attn_part, 'tensor') + b_output.astype(jnp.float32)  224 us
    psum x1, waiting for transfers between devices, shards(): outer_total = lax.psum(outer_part, 'tensor') + b_outer.astype(jnp.float32)  218 us
    psum x1, waiting for transfers between devices, shards(): grad_inputs = grad_resid1 + lax.psum(input_part, 'tensor')  162 us
    unnamed x14, waiting for transfers between devices  116 us
    reduce_scatter x1, waiting for transfers between devices, shards(): lax.psum_scatter(grad_w_outer, 'dp', scatter_dimension=1, tiled=True)  46.8 us
    reduce_scatter x1, waiting for transfers between devices, shards(): lax.psum_scatter(grad_w_inner, 'dp', scatter_dimension=0, tiled=True)  37.2 us
  transfers between devices with their start and end apart: 10, of which 9 were waited for; matrix products, arithmetic and copies ran while one was open for 6% of the time, Pallas kernels for 0%

profile of v1, /device:TPU:0, one launch (start us, length us, event | category | flops | bytes accessed | tf_op | source)
XLA Modules:
  0.0 1491.9 jit_solution(14284575868259604310)
XLA Ops:
  23.1 13.0 while.10
  38.2 4.7 fusion.73
  45.1 223.6 %all-reduce.5.cloned.1.call-done = f32[2048,768]{1,0:T(8,128)} async-done(((f32[2048,768]{1,0:T(8,128)}), f32[2048,768]{1,0:T(8,128)}) %all-reduce.5.cloned.1.call-update) | async-done | bytes 6291472 | tf_op jit(solution)/shard_map/psum | solution.py:159
  268.7 4.6 fusion.72
  276.0 18.3 %multiply_convert_fusion.1 = (bf16[2048,768]{1,0:T(8,128)(2,1)S(1)}, f32[2048,768]{1,0:T(8,128)}, f32[2048,768]{1,0:T(8,128)}) fusion(f32[768]{0:T(1024)S(1)} %copy-done.23, bf16[2048,768]{1,0:T(8,128)(2,1)S(1)} %fusion.58, bf16[768,768]{1,0:T(8,128)(2,1)S(1)} %copy-done), kind=kOutput, calls=%fused_computation.79 | convolution fusion | flops 2519728128 | bytes 20057088 | tf_op jit(solution)/shard_map/dot_general | solution.py:166
  304.6 217.8 %all-reduce.7.cloned.1.call-done = f32[2048,768]{1,0:T(8,128)} async-done(((f32[2048,768]{1,0:T(8,128)}), f32[2048,768]{1,0:T(8,128)}) %all-reduce.7.cloned.1.call-update) | async-done | bytes 6291472 | tf_op jit(solution)/shard_map/psum | solution.py:172
  522.4 5.7 fusion.70
  538.1 9.5 convert_reduce_fusion.2
  549.4 4.5 fusion.75
  554.6 423.6 %all-gather.3.cloned.1.call-done = f32[8192,768]{1,0:T(8,128)} async-done(((f32[2048,768]{1,0:T(8,128)}), f32[8192,768]{1,0:T(8,128)}) %all-gather.3.cloned.1.call-update) | async-done | bytes 25165840 | tf_op jit(solution)/shard_map/all_gather | solution.py:13
  978.2 12.7 reduce_sum.188
  990.9 8.1 multiply_reduce_fusion.2
  999.1 4.6 convert_reduce_fusion.3
  1018.6 28.4 %while.27 = (s32[]{:T(128)}, bf16[4,512,192]{1,2,0:T(8,128)(2,1)}, bf16[4,512,192]{1,2,0:T(8,128)(2,1)}, bf16[4,512,192]{1,2,0:T(8,128)(2,1)}, bf16[4,512,3,64]{...) while((s32[]{:T(128)}, bf16[4,512,192]{1,2,0:T(8,128)(2,1)}, ...), condition=%wide.region_17.18_spmd, body=%wide.region_15.17_spmd.sunk | while | flops 513243648 | bytes 26787972 | solution.py:200
  1055.6 6.9 fusion.78
  1062.8 7.8 fusion.63
  1086.6 26.5 %all-reduce = (f32[192]{0:T(256)}, f32[192]{0:T(256)}, f32[768]{0:T(1024)}, f32[768]{0:T(1024)}, f32[768]{0:T(1024)}, /*index=5*/f32[768]{0:T(1024)}, f32[768]{0:T(1024)}, f32[768]{0:T(1024)}, f32[768]{0:T(1024)}) all-reduce(f32[192]{0:T(256)S(1)} %convert_reduce_fusion.5, ...), channel_id=1, replica_groups=mesh['dp'=8,'tensor'=4] {'dp'}, use_global_device_ids=true, to_apply=%region_21.22 | all-reduce | flops 5760 | bytes 46080 | tf_op jit(solution)/shard_map/psum | solution.py:219
  1114.8 161.9 %all-reduce.9.cloned.1.call-done = f32[2048,768]{1,0:T(8,128)} async-done(((f32[2048,768]{1,0:T(8,128)}), f32[2048,768]{1,0:T(8,128)}) %all-reduce.9.cloned.1.call-update) | async-done | bytes 6291472 | tf_op jit(solution)/shard_map/psum | solution.py:218
  1276.7 8.1 add.175
  1284.8 37.2 %reduce-scatter.15.cloned.1.call-done = f32[96,768]{1,0:T(8,128)} async-done(((f32[768,768]{1,0:T(8,128)}), f32[96,768]{1,0:T(8,128)}) %reduce-scatter.15.cloned.1.call-update) | async-done | bytes 294928 | tf_op jit(solution)/shard_map/reduce_scatter | solution.py:238
  1322.0 46.8 %reduce-scatter.17.cloned.1.call-done = f32[768,96]{0,1:T(8,128)} async-done(((f32[768,768]{0,1:T(8,128)}), f32[768,96]{0,1:T(8,128)}) %reduce-scatter.17.cloned.1.call-update) | async-done | bytes 294928 | tf_op jit(solution)/shard_map/reduce_scatter | solution.py:239
  1368.8 38.7 %reduce-scatter.21.cloned.1.call-done = f32[96,192]{1,0:T(8,128)} async-done(((f32[768,192]{1,0:T(8,128)}), f32[96,192]{1,0:T(8,128)}) %reduce-scatter.21.cloned.1.call-update) | async-done | bytes 73744
  1407.5 38.8 %reduce-scatter.19.cloned.1.call-done = f32[96,192]{1,0:T(8,128)} async-done(((f32[768,192]{1,0:T(8,128)}), f32[96,192]{1,0:T(8,128)}) %reduce-scatter.19.cloned.1.call-update) | async-done | bytes 73744
  1446.3 38.6 %reduce-scatter.23.cloned.1.call-done = f32[96,192]{1,0:T(8,128)} async-done(((f32[768,192]{1,0:T(8,128)}), f32[96,192]{1,0:T(8,128)}) %reduce-scatter.23.cloned.1.call-update) | async-done | bytes 73744
  (204 shorter events, 128.0 us)
Async XLA Ops:
  7.2 268.8 %copy-start = (bf16[768,768]{1,0:T(8,128)(2,1)S(1)}, bf16[768,768]{1,0:T(8,128)(2,1)}, u32[]{:S(2)}) copy-start(bf16[768,768]{1,0:T(8,128)(2,1)} %param.31) | copy-start | bytes 3538948
  7.2 261.5 %all-reduce.5.cloned.1.call-start = ((), (), s32[]{:S(2)}) async-start(), calls=%async_computation.6 | async-start | bytes 12582912 | tf_op jit(solution)/shard_map/psum | solution.py:159
  38.2 6.9 copy-start.28
  43.0 479.4 %all-reduce.7.cloned.1.call-start = ((), (), s32[]{:S(2)}) async-start(), calls=%async_computation.7 | async-start | bytes 12582912 | tf_op jit(solution)/shard_map/psum | solution.py:172
  276.0 18.3 %copy-start.9 = (bf16[2048,768]{1,0:T(8,128)(2,1)}, bf16[2048,768]{1,0:T(8,128)(2,1)S(1)}, u32[]{:S(2)}) copy-start(bf16[2048,768]{1,0:T(8,128)(2,1)S(1)} %fusion.58) | copy-start | bytes 9437188
  276.0 20.0 %copy-start.29 = (bf16[768,768]{1,0:T(8,128)(2,1)S(1)}, bf16[768,768]{1,0:T(8,128)(2,1)}, u32[]{:S(2)}) copy-start(bf16[768,768]{1,0:T(8,128)(2,1)} %param.33) | copy-start | bytes 3538948
  300.4 677.8 %all-gather.3.cloned.1.call-start = ((), (), s32[]{:S(2)}) async-start(), calls=%async_computation.11 | async-start | bytes 31457280 | tf_op jit(solution)/shard_map/all_gather | solution.py:13
  530.0 8.1 slice-start
  538.1 9.5 copy-start.4
  554.0 559.2 %reduce-scatter.25.cloned.1.call-start = ((), (), s32[]{:S(2)}) async-start(), calls=%async_computation.15 | async-start | bytes 884736
  978.2 12.7 copy-start.15
  1012.7 264.0 %all-reduce.9.cloned.1.call-start = ((), (), s32[]{:S(2)}) async-start(), calls=%async_computation.8 | async-start | bytes 12582912 | tf_op jit(solution)/shard_map/psum | solution.py:218
  1018.6 30.9 %copy-start.11 = (bf16[768,192]{0,1:T(8,128)(2,1)S(1)}, bf16[768,192]{0,1:T(8,128)(2,1)}, u32[]{:S(2)}) copy-start(bf16[768,192]{0,1:T(8,128)(2,1)} %param.22) | copy-start | bytes 884740
  1055.5 266.4 %reduce-scatter.15.cloned.1.call-start = ((), (), s32[]{:S(2)}) async-start(), calls=%async_computation.9 | async-start | bytes 2654208 | tf_op jit(solution)/shard_map/reduce_scatter | solution.py:238
  1062.5 306.3 %reduce-scatter.17.cloned.1.call-start = ((), (), s32[]{:S(2)}) async-start(), calls=%async_computation.10 | async-start | bytes 2654208 | tf_op jit(solution)/shard_map/reduce_scatter | solution.py:239
  1070.6 336.9 %reduce-scatter.21.cloned.1.call-start = ((), (), s32[]{:S(2)}) async-start(), calls=%async_computation.13 | async-start | bytes 884736
  1076.4 10.0 copy-start.7
  1076.4 369.9 %reduce-scatter.19.cloned.1.call-start = ((), (), s32[]{:S(2)}) async-start(), calls=%async_computation.12 | async-start | bytes 884736
  1080.0 6.6 copy-start.18
  1080.0 6.6 copy-start.19
  1080.0 6.6 copy-start.20
  1080.0 6.6 copy-start.22
  1082.3 402.5 %reduce-scatter.23.cloned.1.call-start = ((), (), s32[]{:S(2)}) async-start(), calls=%async_computation.14 | async-start | bytes 884736
  1113.1 371.7 %copy-start.1 = (bf16[768,768]{1,0:T(8,128)(2,1)S(1)}, bf16[768,768]{1,0:T(8,128)(2,1)}, u32[]{:S(2)}) copy-start(bf16[768,768]{1,0:T(8,128)(2,1)} %param.31) | copy-start | bytes 3538948
  (21 other events, 62.1 us)
Sparse Core Ops, SparseCore 0:
  43.1 225.5 all-reduce.4
  300.6 221.7 all-reduce.6
  554.1 424.1 all-gather.2
  1012.8 33.2 reduce-scatter.24
  1055.7 220.9 all-reduce.8
  1280.5 41.4 reduce-scatter.14
  1326.3 42.4 reduce-scatter.16
  1372.5 34.9 reduce-scatter.20
  1411.2 34.9 reduce-scatter.18
  1449.8 34.9 reduce-scatter.22
